TPU v7x, 32 devices: a whole 2x2x4 slice. The times are simulated.
32 devices in a mesh: view: 2 (over core), dom: 16 (over z, y, x).
Axes of the slice: x: 2, y: 2, z: 4, core: 2. Of those that a mesh axis runs over, the one named last changes fastest.
Arguments:
- features: bfloat16 [16384, 512], P('dom'), may hold values from -6 to 6
- feat_keep: int32 [2, 512], P('view'), may hold values 0 or 1
- w_first: bfloat16 [512, 512], replicated, may hold values from -0.25 to 0.25
- w_second: bfloat16 [512, 512], replicated, may hold values from -0.25 to 0.25
- adjacency: bfloat16 [2, 1024, 128, 128], P('view', 'dom'), may hold values from 0 to 0.015625
- tile_src: int32 [2, 128, 8], P('view', 'dom'), may hold values from 0 to 8, as said below
- halo_rows: int32 [16, 16, 8], P('dom'), may hold values from 0 to 1023
- halo_live: int32 [16, 16], P('dom'), may hold values from 0 to 8, as said below
- neg_pick: int32 [16, 16, 8], P('dom'), may hold values from 0 to 1023
Outputs:
- node_loss: float32 [2, 16384], P('view', 'dom')
- grad_first: float32 [512, 512], replicated
- grad_second: float32 [512, 512], replicated
Inputs may be any that keep to these rules, and one draw needn't show every extreme that they name: `tile_src`: the last tile of the first block of every partition reads its last halo block. `halo_live`: some receiver gets 8 live rows from every sender.
All inputs are finite; a program needn't handle non-finite values. No bound on the sum of `feat_keep` on one device may be relied on, other than what follows from the above.
Results may differ from a plain program's by a relative error of at most 0.0015.
The roundings to bfloat16 on the way count: a program that leaves them out, or rounds other values in their place, can miss the bound.
Values may be sent and summed in bfloat16 or wider, within the bound.
No kernel may reach another device: no remote copies, remote signals or barrier semaphores. Data moves between devices by JAX's collectives and lax.ppermute only.
A program may use at most 128 MiB of HBM per device.

v0:
```python
import jax
import jax.numpy as jnp
from jax import lax
from jax.sharding import PartitionSpec as P

inv_temp = 5.0
norm_eps = 1e-06


def swapped(array, axis, distance):
    return lax.ppermute(array, axis, [(i, i ^ 1 << distance) for i in range(lax.axis_size(axis))])


def mix_blocks(ext_blocks, tiles, sources, inv_deg):
    picked = ext_blocks[sources]
    summed = jnp.einsum("ntij,ntjw->niw", tiles, picked, preferred_element_type=jnp.float32)
    own_rows = ext_blocks[: sources.shape[0]].astype(jnp.float32)
    return ((own_rows + summed) * inv_deg[:, :, None]).astype(jnp.bfloat16)


def spread_back(grad_mixed, tiles, sources, inv_deg, total_blocks):
    scaled = (grad_mixed * inv_deg[:, :, None]).astype(jnp.bfloat16)
    spread = jnp.einsum("ntij,niw->ntjw", tiles, scaled, preferred_element_type=jnp.float32)
    ext_grad = jnp.zeros((total_blocks, grad_mixed.shape[1], grad_mixed.shape[2]), jnp.float32)
    ext_grad = ext_grad.at[sources].add(spread)
    return ext_grad.at[: sources.shape[0]].add(scaled.astype(jnp.float32))


def contrast(unit, partner, negatives):
    unit_f = unit.astype(jnp.float32)
    partner_f = partner.astype(jnp.float32)
    positive = inv_temp * jnp.sum(unit_f * partner_f, axis=1)
    scores = inv_temp * jnp.dot(unit, negatives.T, preferred_element_type=jnp.float32)
    expo = jnp.exp(scores)
    total = jnp.exp(positive) + jnp.sum(expo, axis=1)
    node_loss = jnp.log(total) - positive
    prob = (expo / total[:, None]).astype(jnp.bfloat16)
    own_share = jnp.exp(positive) / total
    share_less = own_share - 1.0
    g_anchor = inv_temp * (
        share_less[:, None] * partner_f
        + jnp.dot(prob, negatives, preferred_element_type=jnp.float32)
    )
    g_partner = inv_temp * share_less[:, None] * unit_f
    g_neg = inv_temp * jnp.dot(prob.T, unit, preferred_element_type=jnp.float32)
    return (node_loss, g_anchor, g_partner, g_neg, share_less)


def per_device(
    features, feat_keep, w_first, w_second, adjacency, tile_src, halo_rows, halo_live, neg_pick
):
    row_count, feat_width = features.shape
    hid_width = w_first.shape[1]
    block_rows = adjacency.shape[2]
    block_count = tile_src.shape[1]
    tile_count = tile_src.shape[2]
    part_count = lax.axis_size("dom")
    slot_cap = halo_rows.shape[2]
    neg_count = neg_pick.shape[2]
    tiles = adjacency[0].reshape(block_count, tile_count, block_rows, block_rows)
    sources = tile_src[0]
    inv_deg = 1.0 / (1.0 + jnp.sum(tiles.astype(jnp.float32), axis=(1, 3)))
    keep_cols = feat_keep[0].astype(jnp.bfloat16)
    send_rows = halo_rows[0]
    live_slots = lax.broadcasted_iota(jnp.int32, (part_count, slot_cap), 1) < halo_live[0][:, None]
    live_bf = live_slots.astype(jnp.bfloat16)[:, :, None]
    masked = features * keep_cols
    outgoing = masked[send_rows] * live_bf
    incoming = lax.all_to_all(outgoing, "dom", split_axis=0, concat_axis=0, tiled=True).reshape(
        part_count * slot_cap, feat_width
    )
    ext_first = jnp.concatenate([masked, incoming], 0).reshape(-1, block_rows, feat_width)
    mixed_first = mix_blocks(ext_first, tiles, sources, inv_deg).reshape(row_count, feat_width)
    pre_act = jnp.dot(mixed_first, w_first, preferred_element_type=jnp.float32)
    hidden = jnp.maximum(pre_act, 0.0).astype(jnp.bfloat16)
    hidden_out = hidden[send_rows] * live_bf
    hidden_in = lax.all_to_all(hidden_out, "dom", split_axis=0, concat_axis=0, tiled=True).reshape(
        part_count * slot_cap, hid_width
    )
    ext_second = jnp.concatenate([hidden, hidden_in], 0).reshape(-1, block_rows, hid_width)
    mixed_second = mix_blocks(ext_second, tiles, sources, inv_deg).reshape(row_count, hid_width)
    projected = jnp.dot(mixed_second, w_second, preferred_element_type=jnp.float32)
    inv_norm = lax.rsqrt(jnp.sum(projected * projected, axis=1, keepdims=True) + norm_eps)
    normed = projected * inv_norm
    unit = normed.astype(jnp.bfloat16)
    partner = swapped(unit, "view", 0)
    pick_rows = neg_pick[0].reshape(-1)
    neg_out = partner[neg_pick[0]]
    negatives = lax.all_to_all(neg_out, "dom", split_axis=0, concat_axis=0, tiled=True).reshape(
        part_count * neg_count, hid_width
    )
    node_loss, g_anchor, g_partner, g_neg, share_less = contrast(unit, partner, negatives)
    returned = lax.all_to_all(
        g_neg.reshape(part_count, neg_count, hid_width),
        "dom",
        split_axis=0,
        concat_axis=0,
        tiled=True,
    )
    g_partner = g_partner.at[pick_rows].add(returned.reshape(-1, hid_width))
    g_emb = g_anchor + swapped(g_partner, "view", 0)
    inner = jnp.sum(normed * g_emb, axis=1, keepdims=True)
    g_proj = ((g_emb - normed * inner) * inv_norm).astype(jnp.bfloat16)
    grad_second = jnp.einsum("ih,ik->hk", mixed_second, g_proj, preferred_element_type=jnp.float32)
    g_mixed = jnp.einsum("ik,hk->ih", g_proj, w_second, preferred_element_type=jnp.float32)
    ext_grad = spread_back(
        g_mixed.reshape(block_count, block_rows, hid_width),
        tiles,
        sources,
        inv_deg,
        ext_second.shape[0],
    )
    flat_grad = ext_grad.reshape(-1, hid_width)
    halo_grad = flat_grad[row_count:].reshape(part_count, slot_cap, hid_width)
    back_grad = lax.all_to_all(
        halo_grad.astype(jnp.bfloat16), "dom", split_axis=0, concat_axis=0, tiled=True
    ).astype(halo_grad.dtype)
    back_grad = back_grad * live_slots.astype(jnp.float32)[:, :, None]
    g_hidden = flat_grad[:row_count].at[send_rows.reshape(-1)].add(back_grad.reshape(-1, hid_width))
    g_pre = jnp.where(pre_act > 0, g_hidden, 0.0).astype(jnp.bfloat16)
    grad_first = jnp.einsum("if,ih->fh", mixed_first, g_pre, preferred_element_type=jnp.float32)
    summed = lax.psum((grad_first, grad_second), ("view", "dom"))
    return (node_loss[None, :], summed[0], summed[1])


def solution(mesh):
    placed = (
        P("dom", None),
        P("view", None),
        P(),
        P(),
        P("view", "dom", None, None),
        P("view", "dom", None),
        P("dom", None, None),
        P("dom", None),
        P("dom", None, None),
    )
    return jax.shard_map(
        per_device,
        mesh=mesh,
        in_specs=placed,
        out_specs=(P("view", "dom"), P(), P()),
        check_vma=False,
    )
```

profile of v0, /device:TPU:0, one launch (start us, length us, event | category | flops | bytes accessed | tf_op | source)
XLA Modules:
  0.0 339.7 jit_solution(16240361134284853910)
XLA Ops:
  15.5 8.3 %all-to-all-start = ((bf16[16,8,512]{2,1,0:T(8,128)(2,1)}), bf16[16,8,512]{2,1,0:T(8,128)(2,1)S(1)}, u32[]{:S(2)}, u32[]{:S(2)}) async-start(bf16[16,8,512]{2,1,0:T(8,128)(2,1)} %bitcast_multiply_fusion.1), calls=%async_computation | async-start | bytes 262144 | tf_op jit(solution)/shard_map/all_to_all | solution.py:69
  24.6 7.0 %all-to-all-done = bf16[16,8,512]{2,1,0:T(8,128)(2,1)S(1)} async-done(((bf16[16,8,512]{2,1,0:T(8,128)(2,1)}), bf16[16,8,512]{2,1,0:T(8,128)(2,1)S(1)}, u32[]{:S(2)}, u32[]{:S(2)}) %all-to-all-start) | async-done | bytes 131104 | tf_op jit(solution)/shard_map/all_to_all | solution.py:69
  33.0 5.5 %gather_fusion.1 = bf16[64,128,512]{2,1,0:T(8,128)(2,1)} fusion(bf16[9,128,512]{2,1,0:T(8,128)(2,1)S(1)} %bitcast.105, s32[1024]{0:T(1024)S(1)} %pad_clamp_fusion.1), kind=kCustom, calls=%fused_computation.1 | custom fusion | bytes 16777472 | tf_op jit(solution)/shard_map/gather | solution.py:15
  38.5 5.4 %fusion.7 = bf16[8,128,512]{2,1,0:T(8,128)(2,1)S(1)} fusion(bf16[8,128,512]{2,1,0:T(8,128)(2,1)S(1)} %bitcast.114, bf16[8,8,128,128]{3,2,1,0:T(8,128)(2,1)} %bitcast.107, bf16[8,8,128,512]{3,2,1,0:T(8,128)(2,1)} %bitcast.111, f32[8,128]{1,0:T(8,128)S(1)} %add_divide_fusion), kind=kOutput, calls=%fused_computation.23 | convolution fusion | flops 1075838976 | bytes 12587008 | tf_op jit(solution)/shard_map/ntij,ntjw->niw/dot_general | solution.py:16
  46.9 10.4 %all_to_all.25 = bf16[16,8,512]{2,1,0:T(8,128)(2,1)S(1)} all-to-all(bf16[16,8,512]{2,1,0:T(8,128)(2,1)S(1)} %bitcast_multiply_fusion), channel_id=1, replica_groups=mesh['view'=2,'dom'=16] {'dom'}, dimensions={0} | all-to-all | bytes 262144 | tf_op jit(solution)/shard_map/all_to_all | solution.py:77
  57.3 5.5 %gather_fusion.3 = bf16[64,128,512]{2,1,0:T(8,128)(2,1)} fusion(bf16[9,128,512]{2,1,0:T(8,128)(2,1)S(1)} %bitcast.104, s32[1024]{0:T(1024)S(1)} %pad_clamp_fusion.1), kind=kCustom, calls=%fused_computation.3 | custom fusion | bytes 16777472 | tf_op jit(solution)/shard_map/gather | solution.py:15
  62.9 5.3 %fusion.5 = bf16[8,128,512]{2,1,0:T(8,128)(2,1)S(1)} fusion(bf16[8,128,512]{2,1,0:T(8,128)(2,1)S(1)} %bitcast.115, bf16[8,8,128,128]{3,2,1,0:T(8,128)(2,1)} %bitcast.108, bf16[8,8,128,512]{3,2,1,0:T(8,128)(2,1)} %bitcast.110, f32[8,128]{1,0:T(8,128)S(1)} %add_divide_fusion), kind=kOutput, calls=%fused_computation.20 | convolution fusion | flops 1075838976 | bytes 12587008 | tf_op jit(solution)/shard_map/ntij,ntjw->niw/dot_general | solution.py:16
  78.4 3.5 %all-to-all-start.2 = ((bf16[16,8,512]{2,1,0:T(8,128)(2,1)}), bf16[16,8,512]{2,1,0:T(8,128)(2,1)S(1)}, u32[]{:S(2)}, u32[]{:S(2)}) async-start(bf16[16,8,512]{2,1,0:T(8,128)(2,1)} %bitcast.25), calls=%async_computation.2 | async-start | bytes 262144 | tf_op jit(solution)/shard_map/all_to_all | solution.py:89
  84.2 5.7 %all-to-all-done.2 = bf16[16,8,512]{2,1,0:T(8,128)(2,1)S(1)} async-done(((bf16[16,8,512]{2,1,0:T(8,128)(2,1)}), bf16[16,8,512]{2,1,0:T(8,128)(2,1)S(1)}, u32[]{:S(2)}, u32[]{:S(2)}) %all-to-all-start.2) | async-done | bytes 131104 | tf_op jit(solution)/shard_map/all_to_all | solution.py:89
  94.5 3.7 %all-to-all-start.3 = ((f32[16,8,512]{2,1,0:T(8,128)}), f32[16,8,512]{2,1,0:T(8,128)S(1)}, u32[]{:S(2)}, u32[]{:S(2)}) async-start(f32[16,8,512]{2,1,0:T(8,128)} %fusion.9), calls=%async_computation.3 | async-start | bytes 524288 | tf_op jit(solution)/shard_map/all_to_all | solution.py:93
  101.7 2.9 copy.33
  107.4 4.4 %scatter_custom_fusion = f32[1024,512]{1,0:T(8,128)} fusion(f32[1024,512]{1,0:T(8,128)} %copy.33, s32[128]{0:T(128)} %fusion.28, f32[16,8,512]{2,1,0:T(8,128)S(1)} %all-to-all-done.3), kind=kCustom, calls=%fused_computation.45 | custom fusion | flops 65536 | bytes 2359296 | tf_op jit(solution)/shard_map/scatter-add | solution.py:100
  111.7 2.9 copy.34
  114.8 4.3 %collective-permute-done.1 = f32[1024,512]{0,1:T(8,128)} collective-permute-done((f32[1024,512]{0,1:T(8,128)}, f32[1024,512]{0,1:T(8,128)}, u32[]{:S(2)}, u32[]{:S(2)}) %collective-permute-start.1) | collective-permute-done | bytes 2097184 | tf_op jit(solution)/shard_map/ppermute | solution.py:11
  125.4 8.2 %convolution_bitcast_fusion = f32[8,8,128,512]{2,3,1,0:T(8,128)} fusion(bf16[8,8,128,128]{3,2,1,0:T(8,128)(2,1)S(1)} %bitcast.109, f32[8,128,512]{2,1,0:T(8,128)S(1)} %bitcast.112, f32[8,128]{1,0:T(8,128)S(1)} %add_divide_fusion), kind=kOutput, calls=%fused_computation.8 | convolution fusion | flops 1074790400 | bytes 20975616 | tf_op jit(solution)/shard_map/ntij,niw->ntjw/dot_general | solution.py:23
  133.6 16.5 %copy.36 = f32[8,8,128,512]{3,2,1,0:T(8,128)} copy(f32[8,8,128,512]{2,3,1,0:T(8,128)} %convolution_bitcast_fusion) | data formatting | bytes 33554432 | tf_op jit(solution)/shard_map/ntij,niw->ntjw/dot_general | solution.py:23
  150.3 23.0 %scatter_fusion = f32[9,128,512]{2,1,0:T(8,128)S(1)} fusion(f32[9,128,512]{2,1,0:T(8,128)S(1)} %broadcast_in_dim.3, s32[64]{0:T(128)S(1)} %reshape.345, f32[64,128,512]{2,1,0:T(8,128)} %bitcast.106), kind=kCustom, calls=%fused_computation.6 | custom fusion | flops 4194304 | bytes 50331904 | tf_op jit(solution)/shard_map/scatter-add | solution.py:25
  173.4 3.2 slice_add_fusion
  177.3 3.9 %all-to-all-start.4 = ((bf16[16,8,512]{2,1,0:T(8,128)(2,1)}), bf16[16,8,512]{2,1,0:T(8,128)(2,1)S(1)}, u32[]{:S(2)}, u32[]{:S(2)}) async-start(bf16[16,8,512]{2,1,0:T(8,128)(2,1)} %fusion.19), calls=%async_computation.4 | async-start | bytes 262144 | tf_op jit(solution)/shard_map/all_to_all | solution.py:115
  181.2 3.3 fusion.33
  184.6 4.4 %all-to-all-done.4 = bf16[16,8,512]{2,1,0:T(8,128)(2,1)S(1)} async-done(((bf16[16,8,512]{2,1,0:T(8,128)(2,1)}), bf16[16,8,512]{2,1,0:T(8,128)(2,1)S(1)}, u32[]{:S(2)}, u32[]{:S(2)}) %all-to-all-start.4) | async-done | bytes 131104 | tf_op jit(solution)/shard_map/all_to_all | solution.py:115
  189.0 4.3 %scatter_custom_fusion.2 = f32[1024,512]{1,0:T(8,128)} fusion(f32[1024,512]{1,0:T(8,128)} %bitcast.118, s32[128]{0:T(128)S(1)} %fusion.29, bf16[16,8,512]{2,1,0:T(8,128)(2,1)S(1)} %all-to-all-done.4, f32[16,8]{1,0:T(8,128)S(1)} %copy-done.12), kind=kCustom, calls=%fused_computation.43 | custom fusion | flops 196608 | bytes 2236416 | tf_op jit(solution)/shard_map/scatter-add | solution.py:119
  193.3 3.9 %fusion.10 = f32[512,512]{1,0:T(8,128)} fusion(bf16[1024,512]{1,0:T(8,128)(2,1)S(1)} %bitcast.117, f32[1024,512]{1,0:T(8,128)} %scatter_custom_fusion.2, f32[1024,512]{1,0:T(8,128)} %get-tuple-element.24), kind=kOutput, calls=%fused_computation.37 | convolution fusion | flops 537919488 | bytes 6291456 | tf_op jit(solution)/shard_map/if,ih->fh/dot_general | solution.py:121
  198.5 131.0 %all-reduce.3.cloned.1.call-done = (f32[512,512]{1,0:T(8,128)}, f32[512,512]{1,0:T(8,128)}) async-done(((f32[512,512]{1,0:T(8,128)}, f32[512,512]{1,0:T(8,128)}), (f32[512,512]{1,0:T(8,128)}, f32[512,512]{1,0:T(8,128)})) %all-reduce.3.cloned.1.call-update) | async-done | bytes 2097168 | tf_op jit(solution)/shard_map/psum | solution.py:122
  (94 shorter events, 48.7 us)
Async XLA Ops:
  7.2 61.0 %copy-start = (bf16[512,512]{1,0:T(8,128)(2,1)S(1)}, bf16[512,512]{1,0:T(8,128)(2,1)}, u32[]{:S(2)}) copy-start(bf16[512,512]{1,0:T(8,128)(2,1)} %param.14) | copy-start | bytes 1572868
  7.2 16.7 %copy-start.19 = (s32[1,8,8]{2,1,0:T(8,128)S(1)}, s32[1,8,8]{2,1,0:T(8,128)}, u32[]{:S(2)}) copy-start(s32[1,8,8]{2,1,0:T(8,128)} %param.16) | copy-start | bytes 772
  7.2 16.8 %copy-start.2 = (bf16[1,64,128,128]{3,2,1,0:T(8,128)(2,1)S(1)}, bf16[1,64,128,128]{3,2,1,0:T(8,128)(2,1)}, u32[]{:S(2)}) copy-start(bf16[1,64,128,128]{3,2,1,0:T(8,128)(2,1)} %param.15) | copy-start | bytes 6291460
  15.5 16.1 %all-to-all-start = ((bf16[16,8,512]{2,1,0:T(8,128)(2,1)}), bf16[16,8,512]{2,1,0:T(8,128)(2,1)S(1)}, u32[]{:S(2)}, u32[]{:S(2)}) async-start(bf16[16,8,512]{2,1,0:T(8,128)(2,1)} %bitcast_multiply_fusion.1), calls=%async_computation | async-start | bytes 262144 | tf_op jit(solution)/shard_map/all_to_all | solution.py:69
  32.9 5.5 %copy-start.5 = (bf16[1024,512]{1,0:T(8,128)(2,1)S(1)}, bf16[1024,512]{1,0:T(8,128)(2,1)}, u32[]{:S(2)}) copy-start(bf16[1024,512]{1,0:T(8,128)(2,1)} %broadcast_multiply_fusion) | copy-start | bytes 3145732
  38.5 5.4 %copy-start.11 = (bf16[512,512]{1,0:T(8,128)(2,1)S(1)}, bf16[512,512]{1,0:T(8,128)(2,1)}, u32[]{:S(2)}) copy-start(bf16[512,512]{1,0:T(8,128)(2,1)} %param.13) | copy-start | bytes 1572868
  43.8 2.1 copy-start.6
  68.2 2.1 copy-start.8
  70.2 3.0 collective-permute-start
  78.4 11.5 %all-to-all-start.2 = ((bf16[16,8,512]{2,1,0:T(8,128)(2,1)}), bf16[16,8,512]{2,1,0:T(8,128)(2,1)S(1)}, u32[]{:S(2)}, u32[]{:S(2)}) async-start(bf16[16,8,512]{2,1,0:T(8,128)(2,1)} %bitcast.25), calls=%async_computation.2 | async-start | bytes 262144 | tf_op jit(solution)/shard_map/all_to_all | solution.py:89
  92.1 2.4 copy-start.14
  94.5 12.8 %all-to-all-start.3 = ((f32[16,8,512]{2,1,0:T(8,128)}), f32[16,8,512]{2,1,0:T(8,128)S(1)}, u32[]{:S(2)}, u32[]{:S(2)}) async-start(f32[16,8,512]{2,1,0:T(8,128)} %fusion.9), calls=%async_computation.3 | async-start | bytes 524288 | tf_op jit(solution)/shard_map/all_to_all | solution.py:93
  111.7 2.9 copy-start.17
  111.7 7.4 %copy-start.13 = (f32[1024]{0:T(1024)S(1)}, f32[1024]{0:T(1024)}, u32[]{:S(2)}) copy-start(f32[1024]{0:T(1024)} %get-tuple-element.18) | copy-start | bytes 12292
  111.7 7.4 %copy-start.15 = (f32[1024]{0:T(1024)S(1)}, f32[1024]{0:T(1024)}, u32[]{:S(2)}) copy-start(f32[1024]{0:T(1024)} %copy-done.14) | copy-start | bytes 12292
  114.6 4.5 %collective-permute-start.1 = (f32[1024,512]{0,1:T(8,128)}, f32[1024,512]{0,1:T(8,128)}, u32[]{:S(2)}, u32[]{:S(2)}) collective-permute-start(f32[1024,512]{0,1:T(8,128)} %copy.34), channel_id=1, source_target_pairs={{0,16},{16,0},{1,17},{17,1},{2,18},{18,2},{3,19},{19,3},{4,20},{20... | collective-permute-start | bytes 6291464 | tf_op jit(solution)/shard_map/ppermute | solution.py:11
  123.3 2.2 copy-start.3
  124.0 1.4 copy-start.4
  176.6 12.4 %copy-start.12 = (f32[16,8]{1,0:T(8,128)S(1)}, f32[16,8]{1,0:T(8,128)}, u32[]{:S(2)}) copy-start(f32[16,8]{1,0:T(8,128)} %get-tuple-element.21) | copy-start | bytes 1540
  177.3 11.7 %all-to-all-start.4 = ((bf16[16,8,512]{2,1,0:T(8,128)(2,1)}), bf16[16,8,512]{2,1,0:T(8,128)(2,1)S(1)}, u32[]{:S(2)}, u32[]{:S(2)}) async-start(bf16[16,8,512]{2,1,0:T(8,128)(2,1)} %fusion.19), calls=%async_computation.4 | async-start | bytes 262144 | tf_op jit(solution)/shard_map/all_to_all | solution.py:115
  181.2 12.1 %copy-start.7 = (bf16[8,128,512]{2,1,0:T(8,128)(2,1)S(1)}, bf16[8,128,512]{2,1,0:T(8,128)(2,1)}, u32[]{:S(2)}) copy-start(bf16[8,128,512]{2,1,0:T(8,128)(2,1)} %copy-done.6) | copy-start | bytes 3145732
  181.2 148.3 %all-reduce.3.cloned.1.call-start = ((), (), s32[]{:S(2)}) async-start(), calls=%async_computation.5 | async-start | bytes 4194304 | tf_op jit(solution)/shard_map/psum | solution.py:122
  329.5 2.4 copy-start.10
  329.5 3.4 copy-start.1
  (3 other events, 2.9 us)
Sparse Core Ops, SparseCore 0:
  197.3 132.1 all-reduce.2
where the time goes:
time: 341 us; the launch traced here: 340 us
  waiting for transfers between devices  158 us (46%)
  other arithmetic  50.9 us (15%)
  local copies, waits for them, and re-layouts  50.3 us (15%)
  matrix products  36.3 us (11%)
  starting transfers between devices  19.5 us (6%)
  between operations  14.4 us (4%)
  blocking collectives  10.4 us (3%)
    psum x1, waiting for transfers between devices, per_device(): summed = lax.psum((grad_first, grad_second), ('view', 'dom'))  131 us
    scatter-add x1, other arithmetic, spread_back(): ext_grad = ext_grad.at[sources].add(spread)  23 us
    dot_general x1, local copies, waits for them, and re-layouts, spread_back(): jnp.einsum('ntij,niw->ntjw', tiles, scaled, preferred_element_type=jnp.fl...  16.5 us
    gather x2, local copies, waits for them, and re-layouts, mix_blocks(): picked = ext_blocks[sources]  11.1 us
    dot_general x2, matrix products, mix_blocks(): jnp.einsum('ntij,ntjw->niw', tiles, picked, preferred_element_type=jnp.fl...  10.7 us
    all_to_all x1, blocking collectives, per_device(): lax.all_to_all(hidden_out, 'dom', split_axis=0, concat_axis=0, tiled=True)  10.4 us
    all_to_all x1, starting transfers between devices, per_device(): lax.all_to_all(outgoing, 'dom', split_axis=0, concat_axis=0, tiled=True)  8.34 us
    dot_general x1, matrix products, spread_back(): jnp.einsum('ntij,niw->ntjw', tiles, scaled, preferred_element_type=jnp.fl...  8.17 us
  transfers between devices with their start and end apart: 7, of which 7 were waited for; matrix products, arithmetic and copies ran while one was open for 4% of the time, Pallas kernels for 0%

commit v1 on v0

--- a/solution.py
+++ b/solution.py
@@ -119,7 +119,8 @@
     g_hidden = flat_grad[:row_count].at[send_rows.reshape(-1)].add(back_grad.reshape(-1, hid_width))
     g_pre = jnp.where(pre_act > 0, g_hidden, 0.0).astype(jnp.bfloat16)
     grad_first = jnp.einsum("if,ih->fh", mixed_first, g_pre, preferred_element_type=jnp.float32)
-    summed = lax.psum((grad_first, grad_second), ("view", "dom"))
+    half = lax.psum((grad_first, grad_second), "view")
+    summed = lax.psum(half, "dom")
     return (node_loss[None, :], summed[0], summed[1])
 
 

time: 341 us -> 361 us (1.059)
  waiting for transfers between devices: 158 us -> 179 us
    psum x1 -> x2, waiting for transfers between devices: 131 us -> 152 us  [the longest x1 133 us: per_device(): summed = lax.psum(half, 'dom')]
  transfers between devices with their start and end apart: 7 -> 8, of which waited for: 7 -> 8; matrix products, arithmetic and copies ran while one was open for 4% -> 4% of each run, Pallas kernels for 0% -> 0%
where the time goes in v1:
time: 361 us; the launch traced here: 360 us
  waiting for transfers between devices  179 us (50%)
  other arithmetic  50.9 us (14%)
  local copies, waits for them, and re-layouts  49.6 us (14%)
  matrix products  36.3 us (10%)
  starting transfers between devices  19.6 us (5%)
  between operations  14.4 us (4%)
  blocking collectives  10.4 us (3%)
    psum x1, waiting for transfers between devices, per_device(): summed = lax.psum(half, 'dom')  133 us
    scatter-add x1, other arithmetic, spread_back(): ext_grad = ext_grad.at[sources].add(spread)  23 us
    psum x1, waiting for transfers between devices, per_device(): half = lax.psum((grad_first, grad_second), 'view')  19 us
    dot_general x1, local copies, waits for them, and re-layouts, spread_back(): jnp.einsum('ntij,niw->ntjw', tiles, scaled, preferred_element_type=jnp.fl...  16.5 us
    gather x2, local copies, waits for them, and re-layouts, mix_blocks(): picked = ext_blocks[sources]  11 us
    dot_general x2, matrix products, mix_blocks(): jnp.einsum('ntij,ntjw->niw', tiles, picked, preferred_element_type=jnp.fl...  10.6 us
    all_to_all x1, blocking collectives, per_device(): lax.all_to_all(hidden_out, 'dom', split_axis=0, concat_axis=0, tiled=True)  10.4 us
    all_to_all x1, starting transfers between devices, per_device(): lax.all_to_all(outgoing, 'dom', split_axis=0, concat_axis=0, tiled=True)  8.34 us
  transfers between devices with their start and end apart: 8, of which 8 were waited for; matrix products, arithmetic and copies ran while one was open for 4% of the time, Pallas kernels for 0%

profile of v1, /device:TPU:0, one launch (start us, length us, event | category | flops | bytes accessed | tf_op | source)
XLA Modules:
  0.0 359.9 jit_solution(5992195882639328221)
XLA Ops:
  15.5 8.3 %all-to-all-start = ((bf16[16,8,512]{2,1,0:T(8,128)(2,1)}), bf16[16,8,512]{2,1,0:T(8,128)(2,1)S(1)}, u32[]{:S(2)}, u32[]{:S(2)}) async-start(bf16[16,8,512]{2,1,0:T(8,128)(2,1)} %bitcast_multiply_fusion.1), calls=%async_computation | async-start | bytes 262144 | tf_op jit(solution)/shard_map/all_to_all | solution.py:69
  24.6 7.0 %all-to-all-done = bf16[16,8,512]{2,1,0:T(8,128)(2,1)S(1)} async-done(((bf16[16,8,512]{2,1,0:T(8,128)(2,1)}), bf16[16,8,512]{2,1,0:T(8,128)(2,1)S(1)}, u32[]{:S(2)}, u32[]{:S(2)}) %all-to-all-start) | async-done | bytes 131104 | tf_op jit(solution)/shard_map/all_to_all | solution.py:69
  33.0 5.5 %gather_fusion.1 = bf16[64,128,512]{2,1,0:T(8,128)(2,1)} fusion(bf16[9,128,512]{2,1,0:T(8,128)(2,1)S(1)} %bitcast.105, s32[1024]{0:T(1024)S(1)} %pad_clamp_fusion.1), kind=kCustom, calls=%fused_computation.1 | custom fusion | bytes 16777472 | tf_op jit(solution)/shard_map/gather | solution.py:15
  38.5 5.3 %fusion.7 = bf16[8,128,512]{2,1,0:T(8,128)(2,1)S(1)} fusion(bf16[8,128,512]{2,1,0:T(8,128)(2,1)S(1)} %bitcast.114, bf16[8,8,128,128]{3,2,1,0:T(8,128)(2,1)} %bitcast.107, bf16[8,8,128,512]{3,2,1,0:T(8,128)(2,1)} %bitcast.111, f32[8,128]{1,0:T(8,128)S(1)} %add_divide_fusion), kind=kOutput, calls=%fused_computation.23 | convolution fusion | flops 1075838976 | bytes 12587008 | tf_op jit(solution)/shard_map/ntij,ntjw->niw/dot_general | solution.py:16
  46.8 10.4 %all_to_all.25 = bf16[16,8,512]{2,1,0:T(8,128)(2,1)S(1)} all-to-all(bf16[16,8,512]{2,1,0:T(8,128)(2,1)S(1)} %bitcast_multiply_fusion), channel_id=1, replica_groups=mesh['view'=2,'dom'=16] {'dom'}, dimensions={0} | all-to-all | bytes 262144 | tf_op jit(solution)/shard_map/all_to_all | solution.py:77
  57.3 5.5 %gather_fusion.3 = bf16[64,128,512]{2,1,0:T(8,128)(2,1)} fusion(bf16[9,128,512]{2,1,0:T(8,128)(2,1)S(1)} %bitcast.104, s32[1024]{0:T(1024)S(1)} %pad_clamp_fusion.1), kind=kCustom, calls=%fused_computation.3 | custom fusion | bytes 16777472 | tf_op jit(solution)/shard_map/gather | solution.py:15
  62.8 5.3 %fusion.5 = bf16[8,128,512]{2,1,0:T(8,128)(2,1)S(1)} fusion(bf16[8,128,512]{2,1,0:T(8,128)(2,1)S(1)} %bitcast.115, bf16[8,8,128,128]{3,2,1,0:T(8,128)(2,1)} %bitcast.108, bf16[8,8,128,512]{3,2,1,0:T(8,128)(2,1)} %bitcast.110, f32[8,128]{1,0:T(8,128)S(1)} %add_divide_fusion), kind=kOutput, calls=%fused_computation.20 | convolution fusion | flops 1075838976 | bytes 12587008 | tf_op jit(solution)/shard_map/ntij,ntjw->niw/dot_general | solution.py:16
  78.4 3.5 all-to-all-start.2
  84.2 5.7 %all-to-all-done.2 = bf16[16,8,512]{2,1,0:T(8,128)(2,1)S(1)} async-done(((bf16[16,8,512]{2,1,0:T(8,128)(2,1)}), bf16[16,8,512]{2,1,0:T(8,128)(2,1)S(1)}, u32[]{:S(2)}, u32[]{:S(2)}) %all-to-all-start.2) | async-done | bytes 131104 | tf_op jit(solution)/shard_map/all_to_all | solution.py:89
  94.5 3.7 %all-to-all-start.3 = ((f32[16,8,512]{2,1,0:T(8,128)}), f32[16,8,512]{2,1,0:T(8,128)S(1)}, u32[]{:S(2)}, u32[]{:S(2)}) async-start(f32[16,8,512]{2,1,0:T(8,128)} %fusion.9), calls=%async_computation.3 | async-start | bytes 524288 | tf_op jit(solution)/shard_map/all_to_all | solution.py:93
  101.6 2.9 copy.33
  107.3 4.3 %scatter_custom_fusion = f32[1024,512]{1,0:T(8,128)} fusion(f32[1024,512]{1,0:T(8,128)} %copy.33, s32[128]{0:T(128)} %fusion.28, f32[16,8,512]{2,1,0:T(8,128)S(1)} %all-to-all-done.3), kind=kCustom, calls=%fused_computation.45 | custom fusion | flops 65536 | bytes 2359296 | tf_op jit(solution)/shard_map/scatter-add | solution.py:100
  114.8 4.3 %collective-permute-done.1 = f32[1024,512]{0,1:T(8,128)} collective-permute-done((f32[1024,512]{0,1:T(8,128)}, f32[1024,512]{0,1:T(8,128)}, u32[]{:S(2)}, u32[]{:S(2)}) %collective-permute-start.1) | collective-permute-done | bytes 2097184 | tf_op jit(solution)/shard_map/ppermute | solution.py:11
  125.4 8.2 %convolution_bitcast_fusion = f32[8,8,128,512]{2,3,1,0:T(8,128)} fusion(bf16[8,8,128,128]{3,2,1,0:T(8,128)(2,1)S(1)} %bitcast.109, f32[8,128,512]{2,1,0:T(8,128)S(1)} %bitcast.112, f32[8,128]{1,0:T(8,128)S(1)} %add_divide_fusion), kind=kOutput, calls=%fused_computation.8 | convolution fusion | flops 1074790400 | bytes 20975616 | tf_op jit(solution)/shard_map/ntij,niw->ntjw/dot_general | solution.py:23
  133.6 16.5 %copy.36 = f32[8,8,128,512]{3,2,1,0:T(8,128)} copy(f32[8,8,128,512]{2,3,1,0:T(8,128)} %convolution_bitcast_fusion) | data formatting | bytes 33554432 | tf_op jit(solution)/shard_map/ntij,niw->ntjw/dot_general | solution.py:23
  150.3 23.0 %scatter_fusion = f32[9,128,512]{2,1,0:T(8,128)S(1)} fusion(f32[9,128,512]{2,1,0:T(8,128)S(1)} %broadcast_in_dim.3, s32[64]{0:T(128)S(1)} %reshape.345, f32[64,128,512]{2,1,0:T(8,128)} %bitcast.106), kind=kCustom, calls=%fused_computation.6 | custom fusion | flops 4194304 | bytes 50331904 | tf_op jit(solution)/shard_map/scatter-add | solution.py:25
  173.4 3.2 slice_add_fusion
  177.2 3.9 %all-to-all-start.4 = ((bf16[16,8,512]{2,1,0:T(8,128)(2,1)}), bf16[16,8,512]{2,1,0:T(8,128)(2,1)S(1)}, u32[]{:S(2)}, u32[]{:S(2)}) async-start(bf16[16,8,512]{2,1,0:T(8,128)(2,1)} %fusion.19), calls=%async_computation.4 | async-start | bytes 262144 | tf_op jit(solution)/shard_map/all_to_all | solution.py:115
  181.2 3.3 fusion.33
  184.5 4.4 %all-to-all-done.4 = bf16[16,8,512]{2,1,0:T(8,128)(2,1)S(1)} async-done(((bf16[16,8,512]{2,1,0:T(8,128)(2,1)}), bf16[16,8,512]{2,1,0:T(8,128)(2,1)S(1)}, u32[]{:S(2)}, u32[]{:S(2)}) %all-to-all-start.4) | async-done | bytes 131104 | tf_op jit(solution)/shard_map/all_to_all | solution.py:115
  188.9 4.3 %scatter_custom_fusion.2 = f32[1024,512]{1,0:T(8,128)} fusion(f32[1024,512]{1,0:T(8,128)} %bitcast.118, s32[128]{0:T(128)S(1)} %fusion.29, bf16[16,8,512]{2,1,0:T(8,128)(2,1)S(1)} %all-to-all-done.4, f32[16,8]{1,0:T(8,128)S(1)} %copy-done.12), kind=kCustom, calls=%fused_computation.43 | custom fusion | flops 196608 | bytes 2236416 | tf_op jit(solution)/shard_map/scatter-add | solution.py:119
  193.2 3.9 %fusion.10 = f32[512,512]{1,0:T(8,128)} fusion(bf16[1024,512]{1,0:T(8,128)(2,1)S(1)} %bitcast.117, f32[1024,512]{1,0:T(8,128)} %scatter_custom_fusion.2, f32[1024,512]{1,0:T(8,128)} %get-tuple-element.26), kind=kOutput, calls=%fused_computation.37 | convolution fusion | flops 537919488 | bytes 6291456 | tf_op jit(solution)/shard_map/if,ih->fh/dot_general | solution.py:121
  197.2 19.0 %all-reduce.7.cloned.1.call-done = (f32[512,512]{1,0:T(8,128)}, f32[512,512]{1,0:T(8,128)}) async-done(((f32[512,512]{1,0:T(8,128)}, f32[512,512]{1,0:T(8,128)}), (f32[512,512]{1,0:T(8,128)}, f32[512,512]{1,0:T(8,128)})) %all-reduce.7.cloned.1.call-update) | async-done | bytes 2097168 | tf_op jit(solution)/shard_map/psum | solution.py:122
  216.9 132.8 %all-reduce.5.cloned.1.call-done = (f32[512,512]{1,0:T(8,128)}, f32[512,512]{1,0:T(8,128)}) async-done(((f32[512,512]{1,0:T(8,128)}, f32[512,512]{1,0:T(8,128)}), (f32[512,512]{1,0:T(8,128)}, f32[512,512]{1,0:T(8,128)})) %all-reduce.5.cloned.1.call-update) | async-done | bytes 2097168 | tf_op jit(solution)/shard_map/psum | solution.py:123
  (97 shorter events, 51.0 us)
Async XLA Ops:
  7.2 61.0 %copy-start = (bf16[512,512]{1,0:T(8,128)(2,1)S(1)}, bf16[512,512]{1,0:T(8,128)(2,1)}, u32[]{:S(2)}) copy-start(bf16[512,512]{1,0:T(8,128)(2,1)} %param.14) | copy-start | bytes 1572868
  7.2 16.7 %copy-start.19 = (s32[1,8,8]{2,1,0:T(8,128)S(1)}, s32[1,8,8]{2,1,0:T(8,128)}, u32[]{:S(2)}) copy-start(s32[1,8,8]{2,1,0:T(8,128)} %param.16) | copy-start | bytes 772
  7.2 16.8 %copy-start.2 = (bf16[1,64,128,128]{3,2,1,0:T(8,128)(2,1)S(1)}, bf16[1,64,128,128]{3,2,1,0:T(8,128)(2,1)}, u32[]{:S(2)}) copy-start(bf16[1,64,128,128]{3,2,1,0:T(8,128)(2,1)} %param.15) | copy-start | bytes 6291460
  15.5 16.1 %all-to-all-start = ((bf16[16,8,512]{2,1,0:T(8,128)(2,1)}), bf16[16,8,512]{2,1,0:T(8,128)(2,1)S(1)}, u32[]{:S(2)}, u32[]{:S(2)}) async-start(bf16[16,8,512]{2,1,0:T(8,128)(2,1)} %bitcast_multiply_fusion.1), calls=%async_computation | async-start | bytes 262144 | tf_op jit(solution)/shard_map/all_to_all | solution.py:69
  32.9 5.5 %copy-start.5 = (bf16[1024,512]{1,0:T(8,128)(2,1)S(1)}, bf16[1024,512]{1,0:T(8,128)(2,1)}, u32[]{:S(2)}) copy-start(bf16[1024,512]{1,0:T(8,128)(2,1)} %broadcast_multiply_fusion) | copy-start | bytes 3145732
  38.5 5.4 %copy-start.11 = (bf16[512,512]{1,0:T(8,128)(2,1)S(1)}, bf16[512,512]{1,0:T(8,128)(2,1)}, u32[]{:S(2)}) copy-start(bf16[512,512]{1,0:T(8,128)(2,1)} %param.13) | copy-start | bytes 1572868
  43.8 2.1 copy-start.6
  70.2 3.0 collective-permute-start
  78.4 11.5 %all-to-all-start.2 = ((bf16[16,8,512]{2,1,0:T(8,128)(2,1)}), bf16[16,8,512]{2,1,0:T(8,128)(2,1)S(1)}, u32[]{:S(2)}, u32[]{:S(2)}) async-start(bf16[16,8,512]{2,1,0:T(8,128)(2,1)} %bitcast.25), calls=%async_computation.2 | async-start | bytes 262144 | tf_op jit(solution)/shard_map/all_to_all | solution.py:89
  92.0 2.4 copy-start.14
  94.5 12.8 %all-to-all-start.3 = ((f32[16,8,512]{2,1,0:T(8,128)}), f32[16,8,512]{2,1,0:T(8,128)S(1)}, u32[]{:S(2)}, u32[]{:S(2)}) async-start(f32[16,8,512]{2,1,0:T(8,128)} %fusion.9), calls=%async_computation.3 | async-start | bytes 524288 | tf_op jit(solution)/shard_map/all_to_all | solution.py:93
  111.7 2.9 copy-start.17
  111.7 7.4 %copy-start.13 = (f32[1024]{0:T(1024)S(1)}, f32[1024]{0:T(1024)}, u32[]{:S(2)}) copy-start(f32[1024]{0:T(1024)} %get-tuple-element.20) | copy-start | bytes 12292
  111.7 7.4 %copy-start.15 = (f32[1024]{0:T(1024)S(1)}, f32[1024]{0:T(1024)}, u32[]{:S(2)}) copy-start(f32[1024]{0:T(1024)} %copy-done.14) | copy-start | bytes 12292
  114.6 4.5 %collective-permute-start.1 = (f32[1024,512]{0,1:T(8,128)}, f32[1024,512]{0,1:T(8,128)}, u32[]{:S(2)}, u32[]{:S(2)}) collective-permute-start(f32[1024,512]{0,1:T(8,128)} %copy.34), channel_id=1, source_target_pairs={{0,16},{16,0},{1,17},{17,1},{2,18},{18,2},{3,19},{19,3},{4,20},{20... | collective-permute-start | bytes 6291464 | tf_op jit(solution)/shard_map/ppermute | solution.py:11
  123.2 2.2 copy-start.3
  176.6 12.4 %copy-start.12 = (f32[16,8]{1,0:T(8,128)S(1)}, f32[16,8]{1,0:T(8,128)}, u32[]{:S(2)}) copy-start(f32[16,8]{1,0:T(8,128)} %get-tuple-element.23) | copy-start | bytes 1540
  177.2 11.7 %all-to-all-start.4 = ((bf16[16,8,512]{2,1,0:T(8,128)(2,1)}), bf16[16,8,512]{2,1,0:T(8,128)(2,1)S(1)}, u32[]{:S(2)}, u32[]{:S(2)}) async-start(bf16[16,8,512]{2,1,0:T(8,128)(2,1)} %fusion.19), calls=%async_computation.4 | async-start | bytes 262144 | tf_op jit(solution)/shard_map/all_to_all | solution.py:115
  181.1 12.1 %copy-start.7 = (bf16[8,128,512]{2,1,0:T(8,128)(2,1)S(1)}, bf16[8,128,512]{2,1,0:T(8,128)(2,1)}, u32[]{:S(2)}) copy-start(bf16[8,128,512]{2,1,0:T(8,128)(2,1)} %copy-done.6) | copy-start | bytes 3145732
  181.1 35.1 %all-reduce.7.cloned.1.call-start = ((), (), s32[]{:S(2)}) async-start(), calls=%async_computation.6 | async-start | bytes 4194304 | tf_op jit(solution)/shard_map/psum | solution.py:122
  197.2 19.1 %copy-start.18 = (f32[1024]{0:T(1024)S(1)}, f32[1024]{0:T(1024)}, u32[]{:S(2)}) copy-start(f32[1024]{0:T(1024)} %get-tuple-element.22) | copy-start | bytes 12292
  197.2 152.5 %all-reduce.5.cloned.1.call-start = ((), (), s32[]{:S(2)}) async-start(), calls=%async_computation.5 | async-start | bytes 4194304 | tf_op jit(solution)/shard_map/psum | solution.py:123
  349.7 2.4 copy-start.10
  349.7 3.4 copy-start.1
  (4 other events, 5.7 us)
Sparse Core Ops, SparseCore 0:
  197.3 18.9 all-reduce.6
  221.8 127.8 all-reduce.4
